TPU v7x, 128 devices: a whole 4x4x4 slice. The times are simulated.
128 devices in a mesh: row: 64 (over z, y, x), col: 2 (over core).
Axes of the slice: x: 4, y: 4, z: 4, core: 2. Of those that a mesh axis runs over, the one named last changes fastest.
Arguments:
- vectors_in: bfloat16 [131072, 2048], P('row', 'col'), may hold values from -6 to 6
- panel: bfloat16 [131072, 256], P('row', 'col'), may hold values from -0.015625 to 0.015625
- factor: float32 [256, 256], replicated, may hold values from -3 to 8, as said below
- atom_basis: int32 [64, 128], P('row'), may hold values from 1 to 24, 2048 in all within a row
- proj_count: int32 [8192], P('row'), may hold values from 1 to 16
- coupling: bfloat16 [8192, 9, 384], P('row'), may hold values from -0.4375 to 0.4375
- block_present: int32 [8192, 9], P('row'), may hold values 0 or 1
- occ_mask: int32 [2048], P('col'), may hold values 0 or 1
- occ_weight: float32 [2048], P('col'), may hold values from 0.5 to 2
Outputs:
- vectors: bfloat16 [131072, 2048], P('row', 'col')
- density: float32 [8192, 256], P(('row', 'col'))
Inputs may be any that keep to these rules, and one draw needn't show every extreme that they name: `factor`: zero below the diagonal; the diagonal lies in 4 to 8. `atom_basis`: each row sums to 2048, and 24 is reached in each row.
All inputs are finite; a program needn't handle non-finite values. No bound on the sum of `block_present` or of `occ_mask` on one device may be relied on, other than what follows from the above.
Results may differ from a plain program's by a relative error of at most 0.0075.
Values may be sent and summed in bfloat16 or wider, within the bound.
No kernel may reach another device: no remote copies, remote signals or barrier semaphores. Data moves between devices by JAX's collectives and lax.ppermute only.
A program may use at most 192 MiB of HBM per device.

v0:
```python
import jax
import jax.numpy as jnp
from jax import lax
from jax.sharding import PartitionSpec as P

NPMAX = 16
BMAX = 24
K = 9


def with_halo(array, sides, width):
    for axis, dim in sides:
        devices, length = (lax.axis_size(axis), array.shape[dim])
        up = [(i, (i + 1) % devices) for i in range(devices)]
        down = [(j, i) for i, j in up]
        last = lax.slice_in_dim(array, length - width, length, axis=dim)
        first = lax.slice_in_dim(array, 0, width, axis=dim)
        before = lax.ppermute(last, axis, up)
        after = lax.ppermute(first, axis, down)
        array = jnp.concatenate([before, array, after], axis=dim)
    return array


def panel_product(fragment, columns):
    return lax.dot_general(
        fragment, columns, (((0,), (0,)), ((), ())), preferred_element_type=jnp.float32
    )


def local(
    vectors_in, panel, factor, atom_basis, proj_count, coupling, block_present, occ_mask, occ_weight
):
    rows_here = vectors_in.shape[0]
    cols_here = vectors_in.shape[1]
    whole_panel = lax.all_gather(panel, "col", axis=1, tiled=True)
    inner_products = panel_product(whole_panel, vectors_in)
    inner_products = lax.psum(inner_products, "row")
    mixing = jnp.dot(factor.T, inner_products, precision=lax.Precision.HIGHEST).astype(jnp.bfloat16)
    update = jnp.dot(whole_panel, mixing, preferred_element_type=jnp.float32)
    vectors = (vectors_in.astype(jnp.float32) - update).astype(jnp.bfloat16)
    counts = atom_basis[0]
    atoms_here = counts.shape[0]
    starts = jnp.cumsum(counts) - counts
    slot_rank = jnp.arange(BMAX, dtype=jnp.int32)
    row_index = jnp.where(
        slot_rank[None, :] < counts[:, None], starts[:, None] + slot_rank[None, :], rows_here
    )
    padded = jnp.take(vectors, row_index.reshape(-1), axis=0, mode="fill", fill_value=0).reshape(
        atoms_here, BMAX, cols_here
    )
    rim_width = (K - 1) // 2
    extended = with_halo(padded, (("row", 0),), rim_width)
    projections = jnp.zeros((atoms_here, NPMAX, cols_here), jnp.float32)
    for relative in range(K):
        blocks = coupling[:, relative].reshape(atoms_here, NPMAX, BMAX)
        blocks = jnp.where(
            block_present[:, relative, None, None] > 0, blocks, jnp.zeros_like(blocks)
        )
        neighbours = extended[relative : relative + atoms_here]
        projections = projections + jnp.einsum(
            "aij,ajn->ain", blocks, neighbours, preferred_element_type=jnp.float32
        )
    kept_rows = (jnp.arange(NPMAX, dtype=jnp.int32)[None, :] < proj_count[:, None]).astype(
        jnp.float32
    )
    rounded = (projections * kept_rows[:, :, None]).astype(jnp.bfloat16)
    column_total = cols_here * lax.axis_size("col")
    weights = occ_mask.astype(jnp.float32) * occ_weight / column_total
    weighted = (rounded * weights[None, None, :]).astype(jnp.bfloat16)
    partial_value = jnp.einsum(
        "ain,ajn->aij", weighted, rounded, preferred_element_type=jnp.float32
    )
    partial_value = partial_value.reshape(atoms_here, NPMAX * NPMAX)
    summed = lax.psum(partial_value.astype(jnp.bfloat16), "col").astype(jnp.float32)
    per_device = atoms_here // lax.axis_size("col")
    density = lax.dynamic_slice_in_dim(summed, lax.axis_index("col") * per_device, per_device, 0)
    return (vectors, density)


def solution(mesh):
    placed = (
        P("row", "col"),
        P("row", "col"),
        P(),
        P("row", None),
        P("row"),
        P("row", None, None),
        P("row", None),
        P("col"),
        P("col"),
    )
    return jax.shard_map(
        local,
        mesh=mesh,
        in_specs=placed,
        out_specs=(P("row", "col"), P(("row", "col"), None)),
        check_vma=False,
    )
```

profile of v0, /device:TPU:1, one launch (start us, length us, event | category | flops | bytes accessed | tf_op | source)
XLA Modules:
  0.0 322.8 jit_solution(1924844101190805468)
XLA Ops:
  7.2 0.0 copy-start
  7.2 0.0 all-gather.2.cloned.1.call-start
  7.2 0.7 all-gather.2.cloned.1.call-update
  7.9 0.0 all-reduce.3.cloned.1.call-start
  8.0 0.8 copy.17
  8.7 0.2 reduce-window.8
  8.9 0.1 reduce
  9.0 0.7 bitcast_subtract_fusion.1
  9.7 0.8 add_select_fusion
  10.4 0.1 select_n.82
  10.5 0.1 select_n.80
  10.6 1.4 fusion.48
  12.0 0.1 copy.41
  12.1 0.1 copy.42
  12.2 1.0 compare_bitcast_fusion.7
  13.3 0.4 copy.23
  13.7 0.0 copy-start.12
  13.7 0.0 copy-start.10
  13.7 6.4 %copy.15 = bf16[2048,1024]{0,1:T(8,128)(2,1)} copy(bf16[2048,1024]{1,0:T(8,128)(2,1)} %param.9) | data formatting | bytes 8388608 | tf_op args[0]
  20.2 0.1 copy.39
  20.3 0.1 copy.40
  20.5 1.2 copy.19
  21.7 1.2 copy.21
  22.9 0.4 copy.25
  23.3 0.1 copy.44
  23.4 0.1 copy.45
  23.6 1.2 copy.29
  24.8 1.2 copy.31
  26.0 0.1 copy.46
  26.1 0.1 copy.47
  26.3 1.2 copy.33
  27.4 0.4 copy.35
  27.9 0.1 copy.43
  28.0 0.4 copy.27
  28.5 0.1 compare_and_fusion
  28.6 0.0 all-gather.2.cloned.1.call-done
  28.7 4.9 %fusion.51 = f32[256,1024]{1,0:T(8,128)} fusion(bf16[2048,256]{1,0:T(8,128)(2,1)} %all-gather.2.cloned.1.call-done, bf16[2048,1024]{1,0:T(8,128)(2,1)} %param.9), kind=kOutput, calls=%fused_computation.89 | convolution fusion | flops 1073741824 | bytes 6291456 | tf_op jit(solution)/shard_map/dot_general | solution.py:25
  33.5 0.0 all-reduce.3.cloned.1.call-update
  33.6 0.0 all-reduce.5.cloned.1.call-start
  33.7 0.1 fusion.38
  33.7 130.9 %all-reduce.3.cloned.1.call-done = f32[256,1024]{1,0:T(8,128)} async-done(((f32[256,1024]{1,0:T(8,128)}), f32[256,1024]{1,0:T(8,128)}) %all-reduce.3.cloned.1.call-update) | async-done | bytes 1048592 | tf_op jit(solution)/shard_map/psum | solution.py:37
  164.7 3.0 convolution_convert_fusion
  167.7 5.4 %fusion = bf16[2048,1024]{0,1:T(8,128)(2,1)} fusion(bf16[2048,1024]{0,1:T(8,128)(2,1)} %copy.15, bf16[1024,256]{1,0:T(8,128)(2,1)S(1)} %convolution_convert_fusion, bf16[2048,256]{1,0:T(8,128)(2,1)S(1)} %copy-done.4), kind=kOutput, calls=%fused_computation.8 | convolution fusion | flops 1080033280 | bytes 9961472 | tf_op jit(solution)/shard_map/dot_general | solution.py:39
  173.2 6.4 %copy.37 = bf16[2048,1024]{1,0:T(8,128)(2,1)} copy(bf16[2048,1024]{0,1:T(8,128)(2,1)} %fusion) | data formatting | bytes 8388608
  179.5 18.7 %gather_fusion = bf16[3072,1024]{1,0:T(8,128)(2,1)} fusion(bf16[2048,1024]{1,0:T(8,128)(2,1)} %copy.37, s32[3072]{0:T(1024)S(1)} %broadcast_clamp_fusion), kind=kCustom, calls=%fused_computation | custom fusion | bytes 12595200 | tf_op jit(solution)/shard_map/jit(_take)/gather | solution.py:48
  198.2 4.1 %broadcast_select_fusion = bf16[3072,1024]{1,0:T(8,128)(2,1)S(1)} fusion(bf16[3072,1024]{1,0:T(8,128)(2,1)} %gather_fusion, pred[3072]{0:T(1024)(128)(4,1)S(1)} %compare_and_fusion.1), kind=kLoop, calls=%fused_computation.36 | loop fusion | flops 3145728 | bytes 12585984 | tf_op jit(solution)/shard_map/jit(_take)/select_n | solution.py:48
  202.3 0.8 collective-permute-start
  203.1 6.2 %collective-permute-start.1 = (bf16[4,24,1024]{2,1,0:T(8,128)(2,1)S(1)}, bf16[4,24,1024]{2,1,0:T(8,128)(2,1)S(1)}, u32[]{:S(2)}, u32[]{:S(2)}) collective-permute-start(bf16[4,24,1024]{2,1,0:T(8,128)(2,1)S(1)} %bitcast.68), channel_id=1, source_target_pairs={{2,0},{4,2},{6,4},{8,6},{10,8},{12,10},{14,12},{16,14},{18,16},{20... | collective-permute-start | bytes 589832 | tf_op jit(solution)/shard_map/ppermute | solution.py:19
  209.3 0.7 broadcast_select_fusion.1
  210.0 2.3 collective-permute-done
  212.3 4.3 %fusion.12 = f32[128,16,1024]{2,1,0:T(8,128)} fusion(bf16[128,16,24]{2,1,0:T(8,128)(2,1)S(1)} %copy.23, bf16[4,24,1024]{2,1,0:T(8,128)(2,1)S(1)} %collective-permute-done, bf16[128,24,1024]{2,1,0:T(8,128)(2,1)S(1)} %broadcast_select_fusion.1), kind=kOutput, calls=%fused_computation.19 | convolution fusion | flops 103809024 | bytes 14974976 | tf_op jit(solution)/shard_map/aij,ajn->ain/dot_general | solution.py:60
  216.6 4.3 %fusion.15 = f32[128,16,1024]{2,1,0:T(8,128)} fusion(bf16[128,16,24]{2,1,0:T(8,128)(2,1)S(1)} %copy-done.5, bf16[4,24,1024]{2,1,0:T(8,128)(2,1)S(1)} %collective-permute-done, bf16[128,24,1024]{2,1,0:T(8,128)(2,1)S(1)} %broadcast_select_fusion.1), kind=kOutput, calls=%fused_computation.21 | convolution fusion | flops 103809024 | bytes 14974976 | tf_op jit(solution)/shard_map/aij,ajn->ain/dot_general | solution.py:60
  220.9 4.3 %fusion.18 = f32[128,16,1024]{2,1,0:T(8,128)} fusion(bf16[128,16,24]{2,1,0:T(8,128)(2,1)S(1)} %copy-done.6, bf16[4,24,1024]{2,1,0:T(8,128)(2,1)S(1)} %collective-permute-done, bf16[128,24,1024]{2,1,0:T(8,128)(2,1)S(1)} %broadcast_select_fusion.1), kind=kOutput, calls=%fused_computation.23 | convolution fusion | flops 103809024 | bytes 14974976 | tf_op jit(solution)/shard_map/aij,ajn->ain/dot_general | solution.py:60
  225.2 4.3 %fusion.25 = f32[128,16,1024]{2,1,0:T(8,128)} fusion(bf16[128,16,24]{2,1,0:T(8,128)(2,1)S(1)} %copy.25, bf16[128,24,1024]{2,1,0:T(8,128)(2,1)S(1)} %broadcast_select_fusion.1, bf16[4,24,1024]{2,1,0:T(8,128)(2,1)S(1)} %collective-permute-done), kind=kOutput, calls=%fused_computation.31 | convolution fusion | flops 103809024 | bytes 14974976 | tf_op jit(solution)/shard_map/aij,ajn->ain/dot_general | solution.py:60
  229.5 4.3 %fusion.6 = f32[128,16,1024]{2,1,0:T(8,128)} fusion(bf16[128,16,24]{2,1,0:T(8,128)(2,1)S(1)} %copy-done.7, bf16[4,24,1024]{2,1,0:T(8,128)(2,1)S(1)} %collective-permute-done.1, bf16[128,24,1024]{2,1,0:T(8,128)(2,1)S(1)} %broadcast_select_fusion.1), kind=kOutput, calls=%fused_computation.15 | convolution fusion | flops 103809024 | bytes 14974976 | tf_op jit(solution)/shard_map/aij,ajn->ain/dot_general | solution.py:60
  233.8 4.3 %fusion.9 = f32[128,16,1024]{2,1,0:T(8,128)} fusion(bf16[128,16,24]{2,1,0:T(8,128)(2,1)S(1)} %copy-done.8, bf16[4,24,1024]{2,1,0:T(8,128)(2,1)S(1)} %collective-permute-done.1, bf16[128,24,1024]{2,1,0:T(8,128)(2,1)S(1)} %broadcast_select_fusion.1), kind=kOutput, calls=%fused_computation.17 | convolution fusion | flops 103809024 | bytes 14974976 | tf_op jit(solution)/shard_map/aij,ajn->ain/dot_general | solution.py:60
  238.1 4.3 %fusion.3 = f32[128,16,1024]{2,1,0:T(8,128)} fusion(bf16[128,16,24]{2,1,0:T(8,128)(2,1)S(1)} %copy-done.9, bf16[4,24,1024]{2,1,0:T(8,128)(2,1)S(1)} %collective-permute-done.1, bf16[128,24,1024]{2,1,0:T(8,128)(2,1)S(1)} %broadcast_select_fusion.1), kind=kOutput, calls=%fused_computation.13 | convolution fusion | flops 103809024 | bytes 14974976 | tf_op jit(solution)/shard_map/aij,ajn->ain/dot_general | solution.py:60
  242.4 4.3 %fusion.20 = f32[128,16,1024]{2,1,0:T(8,128)} fusion(bf16[128,16,24]{2,1,0:T(8,128)(2,1)S(1)} %copy.35, bf16[4,24,1024]{2,1,0:T(8,128)(2,1)S(1)} %collective-permute-done.1, bf16[128,24,1024]{2,1,0:T(8,128)(2,1)S(1)} %broadcast_select_fusion.1), kind=kOutput, calls=%fused_computation.25 | convolution fusion | flops 103809024 | bytes 14974976 | tf_op jit(solution)/shard_map/aij,ajn->ain/dot_general | solution.py:60
  246.7 46.4 %fusion.37 = bf16[128,16,16]{2,1,0:T(8,128)(2,1)S(1)} fusion(f32[128,16,1024]{2,1,0:T(8,128)} %fusion.20, f32[128,16,1024]{2,1,0:T(8,128)} %fusion.3, f32[128,16,1024]{2,1,0:T(8,128)} %fusion.9, f32[128,16,1024]{2,1,0:T(8,128)} %fusion.6, f32[128,16,1024]{2,1,0:T(8,128)} %fusion.25, f32[128,16,1024]{2,1,0:T(8,128)} %fusion.12, ...), kind=kOutput, calls=%fused_computation.46 | convolution fusion | flops 316702720 | bytes 73576448 | tf_op jit(solution)/shard_map/ain,ajn->aij/dot_general | solution.py:70
  293.0 1.1 copy.36
  294.1 0.0 all-reduce.5.cloned.1.call-update
  294.1 20.5 %all-reduce.5.cloned.1.call-done = bf16[128,256]{0,1:T(8,128)(2,1)} async-done(((bf16[128,256]{0,1:T(8,128)(2,1)}), bf16[128,256]{0,1:T(8,128)(2,1)}) %all-reduce.5.cloned.1.call-update) | async-done | bytes 65552 | tf_op jit(solution)/shard_map/psum | solution.py:74
  314.6 0.9 dynamic-slice_convert_fusion
  315.5 0.7 copy.38
  (36 shorter events, 0.2 us)
Async XLA Ops:
  7.2 157.5 %copy-start = (f32[256,256]{1,0:T(8,128)S(1)}, f32[256,256]{1,0:T(8,128)}, u32[]{:S(2)}) copy-start(f32[256,256]{1,0:T(8,128)} %param.11) | copy-start | bytes 786436
  7.2 21.5 %all-gather.2.cloned.1.call-start = ((), (), s32[]{:S(2)}) async-start(), calls=%async_computation | async-start | bytes 1572864 | tf_op jit(solution)/shard_map/all_gather | solution.py:35
  7.9 156.8 %all-reduce.3.cloned.1.call-start = ((), (), s32[]{:S(2)}) async-start(), calls=%async_computation.1 | async-start | bytes 2097152 | tf_op jit(solution)/shard_map/psum | solution.py:37
  13.7 14.8 %copy-start.11 = (f32[1024]{0:T(1024)S(1)}, f32[1024]{0:T(1024)}, u32[]{:S(2)}) copy-start(f32[1024]{0:T(1024)} %param.17) | copy-start | bytes 12292
  13.7 14.8 %copy-start.12 = (s32[1024]{0:T(1024)S(1)}, s32[1024]{0:T(1024)}, u32[]{:S(2)}) copy-start(s32[1024]{0:T(1024)} %param.16) | copy-start | bytes 12292
  13.7 14.8 %copy-start.10 = (s32[1,128]{1,0:T(1,128)S(1)}, s32[1,128]{1,0:T(1,128)}, u32[]{:S(2)}) copy-start(s32[1,128]{1,0:T(1,128)} %param.12) | copy-start | bytes 1540
  24.8 8.9 %copy-start.13 = (s32[128]{0:T(128)S(1)}, s32[128]{0:T(128)}, u32[]{:S(2)}) copy-start(s32[128]{0:T(128)} %param.13) | copy-start | bytes 1540
  28.7 139.0 %copy-start.4 = (bf16[2048,256]{1,0:T(8,128)(2,1)S(1)}, bf16[2048,256]{1,0:T(8,128)(2,1)}, u32[]{:S(2)}) copy-start(bf16[2048,256]{1,0:T(8,128)(2,1)} %all-gather.2.cloned.1.call-done) | copy-start | bytes 3145732
  33.6 281.0 %all-reduce.5.cloned.1.call-start = ((), (), s32[]{:S(2)}) async-start(), calls=%async_computation.2 | async-start | bytes 131072 | tf_op jit(solution)/shard_map/psum | solution.py:74
  198.2 11.1 %copy-start.3 = (bf16[3072,1024]{1,0:T(8,128)(2,1)S(1)}, bf16[3072,1024]{1,0:T(8,128)(2,1)}, u32[]{:S(2)}) copy-start(bf16[3072,1024]{1,0:T(8,128)(2,1)} %gather_fusion) | copy-start | bytes 18874372
  202.3 10.0 %collective-permute-start = (bf16[4,24,1024]{2,1,0:T(8,128)(2,1)S(1)}, bf16[4,24,1024]{2,1,0:T(8,128)(2,1)S(1)}, u32[]{:S(2)}, u32[]{:S(2)}) collective-permute-start(bf16[4,24,1024]{2,1,0:T(8,128)(2,1)S(1)} %bitcast.69), channel_id=1, source_target_pairs={{0,2},{2,4},{4,6},{6,8},{8,10},{10,12},{12,14},{14,16},{16,18},{18... | collective-permute-start | bytes 589832 | tf_op jit(solution)/shard_map/ppermute | solution.py:18
  203.1 26.4 %collective-permute-start.1 = (bf16[4,24,1024]{2,1,0:T(8,128)(2,1)S(1)}, bf16[4,24,1024]{2,1,0:T(8,128)(2,1)S(1)}, u32[]{:S(2)}, u32[]{:S(2)}) collective-permute-start(bf16[4,24,1024]{2,1,0:T(8,128)(2,1)S(1)} %bitcast.68), channel_id=1, source_target_pairs={{2,0},{4,2},{6,4},{8,6},{10,8},{12,10},{14,12},{16,14},{18,16},{20... | collective-permute-start | bytes 589832 | tf_op jit(solution)/shard_map/ppermute | solution.py:19
  210.0 32.4 %copy-start.2 = (bf16[128,24,1024]{2,1,0:T(8,128)(2,1)}, bf16[128,24,1024]{2,1,0:T(8,128)(2,1)S(1)}, u32[]{:S(2)}) copy-start(bf16[128,24,1024]{2,1,0:T(8,128)(2,1)S(1)} %broadcast_select_fusion.1) | copy-start | bytes 18874372
  210.0 6.6 %copy-start.5 = (bf16[128,16,24]{2,1,0:T(8,128)(2,1)S(1)}, bf16[128,16,24]{2,1,0:T(8,128)(2,1)}, u32[]{:S(2)}) copy-start(bf16[128,16,24]{2,1,0:T(8,128)(2,1)} %copy.19) | copy-start | bytes 294916
  216.6 4.3 %copy-start.6 = (bf16[128,16,24]{2,1,0:T(8,128)(2,1)S(1)}, bf16[128,16,24]{2,1,0:T(8,128)(2,1)}, u32[]{:S(2)}) copy-start(bf16[128,16,24]{2,1,0:T(8,128)(2,1)} %copy.21) | copy-start | bytes 294916
  225.2 4.3 %copy-start.7 = (bf16[128,16,24]{2,1,0:T(8,128)(2,1)S(1)}, bf16[128,16,24]{2,1,0:T(8,128)(2,1)}, u32[]{:S(2)}) copy-start(bf16[128,16,24]{2,1,0:T(8,128)(2,1)} %copy.29) | copy-start | bytes 294916
  229.5 4.3 %copy-start.8 = (bf16[128,16,24]{2,1,0:T(8,128)(2,1)S(1)}, bf16[128,16,24]{2,1,0:T(8,128)(2,1)}, u32[]{:S(2)}) copy-start(bf16[128,16,24]{2,1,0:T(8,128)(2,1)} %copy.31) | copy-start | bytes 294916
  233.8 4.3 %copy-start.9 = (bf16[128,16,24]{2,1,0:T(8,128)(2,1)S(1)}, bf16[128,16,24]{2,1,0:T(8,128)(2,1)}, u32[]{:S(2)}) copy-start(bf16[128,16,24]{2,1,0:T(8,128)(2,1)} %copy.33) | copy-start | bytes 294916
  246.7 69.6 %copy-start.1 = (f32[256,256]{1,0:T(8,128)S(1)}, f32[256,256]{1,0:T(8,128)}, u32[]{:S(2)}) copy-start(f32[256,256]{1,0:T(8,128)} %param.11) | copy-start | bytes 786436
Sparse Core Ops, SparseCore 0:
  9.7 15.3 all-gather.1
  33.7 130.9 all-reduce.2
  294.2 20.3 all-reduce.4
where the time goes:
time: 323 us
  waiting for transfers between devices  154 us (48%)
  matrix products  94 us (29%)
  local copies, waits for them, and re-layouts  44.5 us (14%)
  between operations  14.1 us (4%)
  other arithmetic  8.7 us (3%)
  starting transfers between devices  7.08 us (2%)
    psum x1, waiting for transfers between devices, local(): inner_products = lax.psum(inner_products, 'row')  131 us
    dot_general x1, matrix products, local(): jnp.einsum('ain,ajn->aij', weighted, rounded, preferred_element_type=jnp....  46.4 us
    dot_general x8, matrix products, local(): jnp.einsum('aij,ajn->ain', blocks, neighbours, preferred_element_type=jnp...  34.3 us
    psum x1, waiting for transfers between devices, local(): lax.psum(partial_value.astype(jnp.bfloat16), 'col').astype(jnp.float32)  20.5 us
    gather x1, local copies, waits for them, and re-layouts, local(): jnp.take(vectors, row_index.reshape(-1), axis=0, mode='fill', fill_value=0)  18.7 us
    unnamed x40, local copies, waits for them, and re-layouts  14.7 us
    select_n x9, local copies, waits for them, and re-layouts, local(): jnp.where(block_present[:, relative, None, None] > 0, blocks, jnp.zeros_l...  7.69 us
  transfers between devices with their start and end apart: 5, of which 3 were waited for; matrix products, arithmetic and copies ran while one was open for 12% of the time, Pallas kernels for 0%

commit v1 on v0

--- a/solution.py
+++ b/solution.py
@@ -34,7 +34,7 @@
     cols_here = vectors_in.shape[1]
     whole_panel = lax.all_gather(panel, "col", axis=1, tiled=True)
     inner_products = panel_product(whole_panel, vectors_in)
-    inner_products = lax.psum(inner_products, "row")
+    inner_products = jnp.sum(lax.all_gather(inner_products, "row"), axis=0)
     mixing = jnp.dot(factor.T, inner_products, precision=lax.Precision.HIGHEST).astype(jnp.bfloat16)
     update = jnp.dot(whole_panel, mixing, preferred_element_type=jnp.float32)
     vectors = (vectors_in.astype(jnp.float32) - update).astype(jnp.bfloat16)

time: 323 us -> 486 us (1.50)
  waiting for transfers between devices: 154 us -> 302 us
  other arithmetic: 8.7 us -> 27.2 us
    all_gather x0 -> x1, waiting for transfers between devices: none -> 261 us  [local(): inner_products = jnp.sum(lax.all_gather(inner_products, 'row'), axis=0)]
    psum x1 -> x0, waiting for transfers between devices: 131 us -> none  [local(): inner_products = lax.psum(inner_products, 'row')]
    reduce_sum x0 -> x1, other arithmetic: none -> 20.8 us  [local(): inner_products = jnp.sum(lax.all_gather(inner_products, 'row'), axis=0)]
    all_gather x1, waiting for transfers between devices: 0.02 us -> 17.1 us  [local(): whole_panel = lax.all_gather(panel, 'col', axis=1, tiled=True)]
    unnamed x40 -> x42, local copies, waits for them, and re-layouts: 14.7 us -> 14.8 us
  transfers between devices with their start and end apart: 5 -> 5, of which waited for: 3 -> 4; matrix products, arithmetic and copies ran while one was open for 12% -> 7% of each run, Pallas kernels for 0% -> 0%
where the time goes in v1:
time: 486 us
  waiting for transfers between devices  302 us (62%)
  matrix products  93 us (19%)
  local copies, waits for them, and re-layouts  42.6 us (9%)
  other arithmetic  27.2 us (6%)
  between operations  14.1 us (3%)
  starting transfers between devices  7.08 us (1%)
    all_gather x1, waiting for transfers between devices, local(): inner_products = jnp.sum(lax.all_gather(inner_products, 'row'), axis=0)  261 us
    dot_general x1, matrix products, local(): jnp.einsum('ain,ajn->aij', weighted, rounded, preferred_element_type=jnp....  46.4 us
    dot_general x8, matrix products, local(): jnp.einsum('aij,ajn->ain', blocks, neighbours, preferred_element_type=jnp...  34.3 us
    reduce_sum x1, other arithmetic, local(): inner_products = jnp.sum(lax.all_gather(inner_products, 'row'), axis=0)  20.8 us
    psum x1, waiting for transfers between devices, local(): lax.psum(partial_value.astype(jnp.bfloat16), 'col').astype(jnp.float32)  19.5 us
    gather x1, local copies, waits for them, and re-layouts, local(): jnp.take(vectors, row_index.reshape(-1), axis=0, mode='fill', fill_value=0)  18.6 us
    all_gather x1, waiting for transfers between devices, local(): whole_panel = lax.all_gather(panel, 'col', axis=1, tiled=True)  17.1 us
    unnamed x42, local copies, waits for them, and re-layouts  14.8 us
  transfers between devices with their start and end apart: 5, of which 4 were waited for; matrix products, arithmetic and copies ran while one was open for 7% of the time, Pallas kernels for 0%

profile of v1, /device:TPU:1, one launch (start us, length us, event | category | flops | bytes accessed | tf_op | source)
XLA Modules:
  0.0 485.7 jit_solution(17822947373728774942)
XLA Ops:
  7.2 0.0 copy-start
  7.2 0.0 all-gather.4.cloned.1.call-start
  7.2 0.7 all-gather.4.cloned.1.call-update
  7.9 0.0 all-gather.6.cloned.1.call-start
  8.0 17.1 %all-gather.4.cloned.1.call-done = bf16[2048,256]{1,0:T(8,128)(2,1)} async-done(((bf16[2048,128]{1,0:T(8,128)(2,1)}), bf16[2048,256]{1,0:T(8,128)(2,1)}) %all-gather.4.cloned.1.call-update) | async-done | bytes 1048592 | tf_op jit(solution)/shard_map/all_gather | solution.py:35
  25.0 4.8 fusion.51
  29.8 0.0 all-gather.6.cloned.1.call-update
  29.8 0.0 all-reduce.2.cloned.1.call-start
  29.9 6.5 %copy.15 = bf16[2048,1024]{0,1:T(8,128)(2,1)} copy(bf16[2048,1024]{1,0:T(8,128)(2,1)} %param.9) | data formatting | bytes 8388608 | tf_op args[0]
  36.4 0.0 copy-done.10
  36.4 0.1 copy.17
  36.5 0.2 reduce-window.8
  36.7 0.1 reduce
  36.8 0.1 add_select_fusion
  36.9 0.1 select_n.82
  37.0 0.1 select_n.80
  37.1 0.1 fusion.48
  37.2 0.1 copy.41
  37.4 0.1 copy.42
  37.6 0.4 copy.23
  38.0 0.1 copy.40
  38.1 0.1 copy.39
  38.3 1.2 copy.19
  39.5 1.2 copy.21
  40.8 0.4 copy.25
  41.2 0.1 copy.44
  41.3 0.1 copy.45
  41.5 1.2 copy.29
  42.7 1.2 copy.31
  43.9 0.1 copy.46
  44.0 0.1 copy.47
  44.1 1.2 copy.33
  45.3 0.4 copy.35
  45.8 0.1 copy.43
  45.9 0.4 copy.27
  46.4 0.1 compare_and_fusion
  46.6 0.1 fusion.38
  46.6 260.9 %all-gather.6.cloned.1.call-done = f32[16384,1024]{1,0:T(8,128)} async-done(((f32[256,1024]{1,0:T(8,128)}), f32[16384,1024]{1,0:T(8,128)}) %all-gather.6.cloned.1.call-update) | async-done | bytes 67108880 | tf_op jit(solution)/shard_map/all_gather | solution.py:37
  307.5 20.8 %reduce_sum.9 = f32[256,1024]{1,0:T(8,128)S(1)} reduce(f32[64,256,1024]{2,1,0:T(8,128)} %bitcast, f32[]{:T(128)} %constant.10.clone.1), dimensions={0}, to_apply=%region_0.0 | reduce | flops 16515072 | bytes 68157440 | tf_op jit(solution)/shard_map/reduce_sum | solution.py:37
  328.3 1.8 convolution_convert_fusion
  330.1 5.8 %fusion = bf16[2048,1024]{0,1:T(8,128)(2,1)} fusion(bf16[2048,1024]{0,1:T(8,128)(2,1)} %copy.15, bf16[1024,256]{1,0:T(8,128)(2,1)S(1)} %convolution_convert_fusion, bf16[2048,256]{1,0:T(8,128)(2,1)} %all-gather.4.cloned.1.call-done), kind=kOutput, calls=%fused_computation.8 | convolution fusion | flops 1080033280 | bytes 9961472 | tf_op jit(solution)/shard_map/dot_general | solution.py:39
  335.9 6.4 %copy.37 = bf16[2048,1024]{1,0:T(8,128)(2,1)} copy(bf16[2048,1024]{0,1:T(8,128)(2,1)} %fusion) | data formatting | bytes 8388608
  342.3 18.6 %gather_fusion = bf16[3072,1024]{1,0:T(8,128)(2,1)} fusion(bf16[2048,1024]{1,0:T(8,128)(2,1)} %copy.37, s32[3072]{0:T(1024)S(1)} %broadcast_clamp_fusion), kind=kCustom, calls=%fused_computation | custom fusion | bytes 12595200 | tf_op jit(solution)/shard_map/jit(_take)/gather | solution.py:48
  360.8 4.1 broadcast_select_fusion
  364.9 1.3 collective-permute-start
  366.2 5.7 %collective-permute-start.1 = (bf16[4,24,1024]{2,1,0:T(8,128)(2,1)S(1)}, bf16[4,24,1024]{2,1,0:T(8,128)(2,1)S(1)}, u32[]{:S(2)}, u32[]{:S(2)}) collective-permute-start(bf16[4,24,1024]{2,1,0:T(8,128)(2,1)S(1)} %bitcast.69), channel_id=1, source_target_pairs={{2,0},{4,2},{6,4},{8,6},{10,8},{12,10},{14,12},{16,14},{18,16},{20... | collective-permute-start | bytes 589832 | tf_op jit(solution)/shard_map/ppermute | solution.py:19
  371.9 0.7 broadcast_select_fusion.1
  372.6 3.6 collective-permute-done
  376.2 4.3 fusion.12
  380.5 4.2 fusion.15
  384.8 4.3 fusion.18
  389.1 4.3 fusion.25
  393.4 0.0 collective-permute-done.1
  393.4 4.3 fusion.6
  397.7 4.3 fusion.9
  402.0 4.3 fusion.3
  406.3 0.0 copy-done.2
  406.3 4.3 fusion.20
  410.5 46.4 %fusion.37 = bf16[128,16,16]{2,1,0:T(8,128)(2,1)S(1)} fusion(f32[128,16,1024]{2,1,0:T(8,128)} %fusion.20, f32[128,16,1024]{2,1,0:T(8,128)} %fusion.3, f32[128,16,1024]{2,1,0:T(8,128)} %fusion.9, f32[128,16,1024]{2,1,0:T(8,128)} %fusion.6, f32[128,16,1024]{2,1,0:T(8,128)} %fusion.25, f32[128,16,1024]{2,1,0:T(8,128)} %fusion.12, ...), kind=kOutput, calls=%fused_computation.46 | convolution fusion | flops 316702720 | bytes 73576448 | tf_op jit(solution)/shard_map/ain,ajn->aij/dot_general | solution.py:70
  456.9 1.1 copy.36
  458.0 0.0 all-reduce.2.cloned.1.call-update
  458.0 19.5 %all-reduce.2.cloned.1.call-done = bf16[128,256]{0,1:T(8,128)(2,1)} async-done(((bf16[128,256]{0,1:T(8,128)(2,1)}), bf16[128,256]{0,1:T(8,128)(2,1)}) %all-reduce.2.cloned.1.call-update) | async-done | bytes 65552 | tf_op jit(solution)/shard_map/psum | solution.py:74
  477.5 0.9 dynamic-slice_convert_fusion
  478.4 0.7 copy.38
  (39 shorter events, 0.2 us)
Async XLA Ops:
  7.2 321.1 %copy-start = (f32[256,256]{1,0:T(8,128)S(1)}, f32[256,256]{1,0:T(8,128)}, u32[]{:S(2)}) copy-start(f32[256,256]{1,0:T(8,128)} %param.11) | copy-start | bytes 786436
  7.2 17.9 %all-gather.4.cloned.1.call-start = ((), (), s32[]{:S(2)}) async-start(), calls=%async_computation | async-start | bytes 1572864 | tf_op jit(solution)/shard_map/all_gather | solution.py:35
  7.9 299.6 %all-gather.6.cloned.1.call-start = ((), (), s32[]{:S(2)}) async-start(), calls=%async_computation.2 | async-start | bytes 68157440 | tf_op jit(solution)/shard_map/all_gather | solution.py:37
  29.8 6.6 %copy-start.10 = (s32[1,128]{1,0:T(1,128)S(1)}, s32[1,128]{1,0:T(1,128)}, u32[]{:S(2)}) copy-start(s32[1,128]{1,0:T(1,128)} %param.12) | copy-start | bytes 1540
  29.8 7.3 %copy-start.4 = (bf16[128,9,384]{2,0,1:T(8,128)(2,1)S(1)}, bf16[128,9,384]{2,0,1:T(8,128)(2,1)}, u32[]{:S(2)}) copy-start(bf16[128,9,384]{2,0,1:T(8,128)(2,1)} %param.14) | copy-start | bytes 2654212
  29.8 7.7 %copy-start.13 = (s32[128,9]{0,1:T(8,128)S(1)}, s32[128,9]{0,1:T(8,128)}, u32[]{:S(2)}) copy-start(s32[128,9]{0,1:T(8,128)} %param.15) | copy-start | bytes 13828
  29.8 447.7 %all-reduce.2.cloned.1.call-start = ((), (), s32[]{:S(2)}) async-start(), calls=%async_computation.1 | async-start | bytes 131072 | tf_op jit(solution)/shard_map/psum | solution.py:74
  36.4 9.9 %copy-start.11 = (f32[1024]{0:T(1024)S(1)}, f32[1024]{0:T(1024)}, u32[]{:S(2)}) copy-start(f32[1024]{0:T(1024)} %param.17) | copy-start | bytes 12292
  36.4 10.0 %copy-start.12 = (s32[1024]{0:T(1024)S(1)}, s32[1024]{0:T(1024)}, u32[]{:S(2)}) copy-start(s32[1024]{0:T(1024)} %param.16) | copy-start | bytes 12292
  36.4 10.1 %copy-start.14 = (s32[128]{0:T(128)S(1)}, s32[128]{0:T(128)}, u32[]{:S(2)}) copy-start(s32[128]{0:T(128)} %param.13) | copy-start | bytes 1540
  360.8 11.1 %copy-start.3 = (bf16[3072,1024]{1,0:T(8,128)(2,1)S(1)}, bf16[3072,1024]{1,0:T(8,128)(2,1)}, u32[]{:S(2)}) copy-start(bf16[3072,1024]{1,0:T(8,128)(2,1)} %gather_fusion) | copy-start | bytes 18874372
  364.9 11.3 %collective-permute-start = (bf16[4,24,1024]{2,1,0:T(8,128)(2,1)S(1)}, bf16[4,24,1024]{2,1,0:T(8,128)(2,1)S(1)}, u32[]{:S(2)}, u32[]{:S(2)}) collective-permute-start(bf16[4,24,1024]{2,1,0:T(8,128)(2,1)S(1)} %bitcast.70), channel_id=1, source_target_pairs={{0,2},{2,4},{4,6},{6,8},{8,10},{10,12},{12,14},{14,16},{16,18},{18... | collective-permute-start | bytes 589832 | tf_op jit(solution)/shard_map/ppermute | solution.py:18
  366.2 27.2 %collective-permute-start.1 = (bf16[4,24,1024]{2,1,0:T(8,128)(2,1)S(1)}, bf16[4,24,1024]{2,1,0:T(8,128)(2,1)S(1)}, u32[]{:S(2)}, u32[]{:S(2)}) collective-permute-start(bf16[4,24,1024]{2,1,0:T(8,128)(2,1)S(1)} %bitcast.69), channel_id=1, source_target_pairs={{2,0},{4,2},{6,4},{8,6},{10,8},{12,10},{14,12},{16,14},{18,16},{20... | collective-permute-start | bytes 589832 | tf_op jit(solution)/shard_map/ppermute | solution.py:19
  372.6 33.7 %copy-start.2 = (bf16[128,24,1024]{2,1,0:T(8,128)(2,1)}, bf16[128,24,1024]{2,1,0:T(8,128)(2,1)S(1)}, u32[]{:S(2)}) copy-start(bf16[128,24,1024]{2,1,0:T(8,128)(2,1)S(1)} %broadcast_select_fusion.1) | copy-start | bytes 18874372
  372.6 7.9 %copy-start.5 = (bf16[128,16,24]{2,1,0:T(8,128)(2,1)S(1)}, bf16[128,16,24]{2,1,0:T(8,128)(2,1)}, u32[]{:S(2)}) copy-start(bf16[128,16,24]{2,1,0:T(8,128)(2,1)} %copy.19) | copy-start | bytes 294916
  380.5 4.2 copy-start.6
  389.1 4.3 copy-start.7
  393.4 4.3 copy-start.8
  397.7 4.3 copy-start.9
  410.5 68.6 %copy-start.1 = (f32[256,256]{1,0:T(8,128)S(1)}, f32[256,256]{1,0:T(8,128)}, u32[]{:S(2)}) copy-start(f32[256,256]{1,0:T(8,128)} %param.11) | copy-start | bytes 786436
Sparse Core Ops, SparseCore 0:
  9.7 15.3 all-gather.3
  30.0 277.5 all-gather.5
  458.1 19.3 all-reduce.1
